TPU v7x, 512 devices: a whole 4x4x16 slice. The times are simulated.
512 devices in a mesh: seq: 128 (over y, x_lo, z), tp: 4 (over x_hi, core).
Axes of the slice: x: 4 (x_hi: 2, x_lo: 2; x = x_hi * 2 + x_lo), y: 4, z: 16, core: 2. Of those that a mesh axis runs over, the one named last changes fastest.
Arguments:
- query: bfloat16 [24576, 2560], P('seq', 'tp'), may hold values from -9 to 9
- keys: bfloat16 [28672, 2560], P('seq', 'tp'), may hold values from -9 to 9
- values: bfloat16 [28672, 2560], P('seq', 'tp'), may hold values from -6 to 6
- q_gain: float32 [64], replicated, may hold values from 1.8 to 7
- k_gain: float32 [2, 64], replicated, may hold values from 1.8 to 7
- residual: bfloat16 [24576, 2432], P('seq', 'tp'), may hold values from -6 to 6
- gate: bfloat16 [8, 2432], P(None, 'tp'), may hold values from -5 to 5
- out_weight: bfloat16 [2560, 2432], P('tp'), may hold values from -0.125 to 0.125
- image_count: int32 [8], replicated, may hold values from 1536 to 3072, as said below
Outputs:
- updated: bfloat16 [24576, 2432], P('seq', 'tp')
Inputs may be any that keep to these rules, and one draw needn't show every extreme that they name: Request g's live image tokens are its first image_count[g] image slots; in every draw some request has all 3072 live.
All inputs are finite; a program needn't handle non-finite values.
Results may differ from a plain program's by a relative error of at most 0.025.
Values may be sent and summed in bfloat16 or wider, within the bound.
A program may use at most 128 MiB of HBM per device.

v0:
```python
import jax
import jax.numpy as jnp
from jax import lax
from jax.sharding import PartitionSpec as P

HEADS = 38
HEAD_DIM = 64


epsilon = 1e-06


def from_partner(value, axis, bit):
    mask = 2**bit
    pairs = [(source, source ^ mask) for source in range(lax.axis_size(axis))]
    return lax.ppermute(value, axis, pairs)


def rms_scale(values_in, gain_rows):
    inverse = lax.rsqrt(jnp.mean(values_in * values_in, axis=-1, keepdims=True) + epsilon)
    return values_in * inverse * gain_rows


def local(query, keys, values, q_gain, k_gain, residual, gate, out_weight, image_count):
    seq_devices = lax.axis_size("seq")
    tp_devices = lax.axis_size("tp")
    group_size = min(16, seq_devices // 2)
    bit_total = group_size.bit_length() - 1
    position = lax.axis_index("seq")
    request = position // group_size
    rank_self = position % group_size
    tp_rank = lax.axis_index("tp")
    img_rows = query.shape[0]
    kv_rows = keys.shape[0]
    local_width = query.shape[1]
    heads_here = local_width // HEAD_DIM
    query_float = query.astype(jnp.float32).reshape(img_rows, heads_here, HEAD_DIM)
    query_normed = (
        rms_scale(query_float, q_gain).astype(jnp.bfloat16).reshape(img_rows, local_width)
    )
    text_rows = jnp.arange(kv_rows, dtype=jnp.int32) >= img_rows
    key_gain_rows = jnp.where(text_rows[:, None], k_gain[1][None, :], k_gain[0][None, :])
    key_float = keys.astype(jnp.float32).reshape(kv_rows, heads_here, HEAD_DIM)
    key_normed = (
        rms_scale(key_float, key_gain_rows[:, None, :])
        .astype(jnp.bfloat16)
        .reshape(kv_rows, local_width)
    )
    key_value = jnp.stack([key_normed, values])[:, None]
    block_ranks = jnp.reshape(rank_self, (1,))
    bit_order = list(range(bit_total))
    for bit_index in bit_order:
        partner = from_partner(key_value, "seq", bit_index)
        key_value = jnp.concatenate([key_value, partner], axis=1)
        block_ranks = jnp.concatenate([block_ranks, jnp.bitwise_xor(block_ranks, 1 << bit_index)])
    keys_all = key_value[0].reshape(group_size * kv_rows, local_width)
    values_all = key_value[1].reshape(group_size * kv_rows, local_width)
    live_count = lax.dynamic_index_in_dim(image_count, request, 0, keepdims=False)
    within = jnp.arange(kv_rows, dtype=jnp.int32)
    live = (within[None, :] >= img_rows) | (
        block_ranks[:, None] * img_rows + within[None, :] < live_count
    )
    live = live.reshape(group_size * kv_rows)
    score_scale = HEAD_DIM ** (-0.5)

    def one_head(head_index):
        column = head_index * HEAD_DIM
        query_head = lax.dynamic_slice_in_dim(query_normed, column, HEAD_DIM, 1)
        key_head = lax.dynamic_slice_in_dim(keys_all, column, HEAD_DIM, 1)
        value_head = lax.dynamic_slice_in_dim(values_all, column, HEAD_DIM, 1)
        scores = (
            lax.dot_general(
                query_head, key_head, (((1,), (1,)), ((), ())), preferred_element_type=jnp.float32
            )
            * score_scale
        )
        scores = jnp.where(live[None, :], scores, -1e30)
        maxima = jnp.max(scores, axis=1, keepdims=True)
        expd = jnp.exp(scores - maxima)
        weights = (expd / jnp.sum(expd, axis=1, keepdims=True)).astype(jnp.bfloat16)
        return jnp.dot(weights, value_head, preferred_element_type=jnp.float32)

    heads_out = lax.map(one_head, jnp.arange(heads_here, dtype=jnp.int32))
    head_limit = (HEADS + tp_devices - 1 - tp_rank) // tp_devices
    head_valid = (jnp.arange(heads_here, dtype=jnp.int32) < head_limit).astype(jnp.float32)
    heads_out = heads_out * head_valid[:, None, None]
    attended = (
        jnp.transpose(heads_out, (1, 0, 2)).reshape(img_rows, local_width).astype(jnp.bfloat16)
    )
    share = lax.psum_scatter(
        lax.dot_general(
            out_weight, attended, (((0,), (1,)), ((), ())), preferred_element_type=jnp.float32
        ).astype(jnp.bfloat16),
        "tp",
        scatter_dimension=0,
        tiled=True,
    ).astype(jnp.float32)
    projected = jnp.transpose(share)
    gate_row = lax.dynamic_index_in_dim(gate, request, 0, keepdims=False).astype(jnp.float32)
    return (residual.astype(jnp.float32) + gate_row[None, :] * projected).astype(jnp.bfloat16)


def solution(mesh):
    placed = (
        P("seq", "tp"),
        P("seq", "tp"),
        P("seq", "tp"),
        P(),
        P(),
        P("seq", "tp"),
        P(None, "tp"),
        P("tp", None),
        P(),
    )
    return jax.shard_map(
        local, mesh=mesh, in_specs=placed, out_specs=P("seq", "tp"), check_vma=False
    )
```

profile of v0, /device:TPU:1, one launch (start us, length us, event | category | flops | bytes accessed | tf_op | source)
XLA Modules:
  0.0 963.3 jit_solution(4470212473320839285)
XLA Ops:
  7.4 1.2 copy.21
  10.7 1.9 copy.22
  12.7 2.0 maximum_bitcast_fusion
  14.7 2.1 copy.28
  16.8 4.4 collective-permute-start
  21.2 8.5 collective-permute-done
  29.7 2.1 copy.24
  31.8 2.6 pad_maximum_fusion.2
  34.4 2.4 copy.25
  36.8 9.4 collective-permute-start.1
  46.2 49.5 %collective-permute-done.1 = bf16[2,2,224,640]{3,2,1,0:T(8,128)(2,1)S(1)} collective-permute-done((bf16[2,2,224,640]{3,2,1,0:T(8,128)(2,1)}, bf16[2,2,224,640]{3,2,1,0:T(8,128)(2,1)S(1)}, u32[]{:S(2)}, u32[]{:S(2)}) %collective-permute-start.1) | collective-permute-done | bytes 1146912 | tf_op jit(solution)/shard_map/ppermute | solution.py:16
  95.7 1.9 pad_maximum_fusion.1
  97.7 8.8 collective-permute-start.2
  106.5 295.7 %collective-permute-done.2 = bf16[2,4,224,640]{3,2,1,0:T(8,128)(2,1)S(1)} collective-permute-done((bf16[2,4,224,640]{3,2,1,0:T(8,128)(2,1)S(1)}, bf16[2,4,224,640]{3,2,1,0:T(8,128)(2,1)S(1)}, u32[]{:S(2)}, u32[]{:S(2)}) %collective-permute-start.2) | collective-permute-done | bytes 2293792 | tf_op jit(solution)/shard_map/ppermute | solution.py:16
  402.2 3.5 pad_maximum_fusion
  405.7 210.0 %collective-permute-start.3 = (bf16[2,8,224,640]{3,2,1,0:T(8,128)(2,1)}, bf16[2,8,224,640]{3,2,1,0:T(8,128)(2,1)}, u32[]{:S(2)}, u32[]{:S(2)}) collective-permute-start(bf16[2,8,224,640]{3,2,1,0:T(8,128)(2,1)} %pad_maximum_fusion), channel_id=1, source_target_pairs={{0,32},{4,36},{8,40},{12,44},{16,48},{20,52},{24,56},{28,60},{32,0... | collective-permute-start | bytes 13762568 | tf_op jit(solution)/shard_map/ppermute | solution.py:16
  620.9 2.1 constant_dynamic-update-slice_fusion.4
  623.0 2.0 constant_dynamic-update-slice_fusion.3
  626.0 1.6 constant_dynamic-update-slice_fusion.1
  627.6 186.0 %collective-permute-done.3 = bf16[2,8,224,640]{3,2,1,0:T(8,128)(2,1)} collective-permute-done((bf16[2,8,224,640]{3,2,1,0:T(8,128)(2,1)}, bf16[2,8,224,640]{3,2,1,0:T(8,128)(2,1)}, u32[]{:S(2)}, u32[]{:S(2)}) %collective-permute-start.3) | collective-permute-done | bytes 4587552 | tf_op jit(solution)/shard_map/ppermute | solution.py:16
  813.7 4.8 constant_dynamic-update-slice_fusion
  818.5 8.1 fusion.20
  826.6 77.7 %while.11 = (s32[]{:T(128)}, f32[10,192,64]{1,2,0:T(8,128)}, s32[10]{0:T(128)S(1)}, bf16[192,640]{0,1:T(8,128)(2,1)}, bf16[3584,640]{1,0:T(8,128)(2,1)}, /*index...) while((s32[]{:T(128)}, f32[10,192,64]{1,2,0:T(8,128)}, ...), condition=%wide.region_5.6_spmd.clone, body=%wide.region_2.5_spmd.clone.sunk | while | flops 181676160 | bytes 10211039 | solution.py:83
  828.8 2.1 fusion.30
  831.4 2.9 fusion.32
  836.6 2.1 fusion.30
  839.2 2.9 fusion.32
  844.4 2.1 fusion.30
  847.0 2.9 fusion.32
  852.1 2.1 fusion.30
  854.7 2.9 fusion.32
  859.9 2.1 fusion.30
  862.5 2.9 fusion.32
  867.7 2.1 fusion.30
  870.3 2.9 fusion.32
  875.4 2.1 fusion.30
  878.1 2.9 fusion.32
  883.2 2.1 fusion.30
  885.8 3.0 fusion.32
  891.0 2.1 fusion.30
  893.6 2.9 fusion.32
  898.8 2.1 fusion.30
  901.4 2.9 fusion.32
  904.3 1.2 multiply_convert_fusion
  905.5 2.0 fusion.13
  907.5 2.3 copy.30
  910.6 43.0 %reduce-scatter.4.cloned.1.call-done = bf16[608,192]{1,0:T(8,128)(2,1)} async-done(((bf16[2432,192]{1,0:T(8,128)(2,1)}), bf16[608,192]{1,0:T(8,128)(2,1)}) %reduce-scatter.4.cloned.1.call-update) | async-done | bytes 233488
  954.7 1.7 fusion.18
  (84 shorter events, 31.6 us)
Async XLA Ops:
  6.5 899.0 %copy-start = (bf16[640,2432]{1,0:T(8,128)(2,1)S(1)}, bf16[640,2432]{1,0:T(8,128)(2,1)}, u32[]{:S(2)}) copy-start(bf16[640,2432]{1,0:T(8,128)(2,1)} %param.18) | copy-start | bytes 9338884
  6.5 947.0 %reduce-scatter.4.cloned.1.call-start = ((), (), s32[]{:S(2)}) async-start(), calls=%async_computation.1 | async-start | bytes 1556480
  16.8 12.9 %collective-permute-start = (bf16[2,1,224,640]{3,2,1,0:T(8,128)(2,1)}, bf16[2,1,224,640]{3,2,1,0:T(8,128)(2,1)}, u32[]{:S(2)}, u32[]{:S(2)}) collective-permute-start(bf16[2,1,224,640]{3,2,1,0:T(8,128)(2,1)} %copy.28), channel_id=1, source_target_pairs={{0,4},{4,0},{8,12},{12,8},{16,20},{20,16},{24,28},{28,24},{32,36},... | collective-permute-start | bytes 1720328 | tf_op jit(solution)/shard_map/ppermute | solution.py:16
  36.8 365.4 %copy-start.3 = (bf16[2,1,224,640]{3,2,1,0:T(8,128)(2,1)S(1)}, bf16[2,1,224,640]{3,2,1,0:T(8,128)(2,1)}, u32[]{:S(2)}) copy-start(bf16[2,1,224,640]{3,2,1,0:T(8,128)(2,1)} %copy.28) | copy-start | bytes 1720324
  36.8 58.9 %collective-permute-start.1 = (bf16[2,2,224,640]{3,2,1,0:T(8,128)(2,1)}, bf16[2,2,224,640]{3,2,1,0:T(8,128)(2,1)S(1)}, u32[]{:S(2)}, u32[]{:S(2)}) collective-permute-start(bf16[2,2,224,640]{3,2,1,0:T(8,128)(2,1)} %copy.25), channel_id=1, source_target_pairs={{0,8},{4,12},{8,0},{12,4},{16,24},{20,28},{24,16},{28,20},{32,40},... | collective-permute-start | bytes 3440648 | tf_op jit(solution)/shard_map/ppermute | solution.py:16
  95.7 310.0 %copy-start.1 = (bf16[2,2,224,640]{3,2,1,0:T(8,128)(2,1)}, bf16[2,2,224,640]{3,2,1,0:T(8,128)(2,1)S(1)}, u32[]{:S(2)}) copy-start(bf16[2,2,224,640]{3,2,1,0:T(8,128)(2,1)S(1)} %collective-permute-done.1) | copy-start | bytes 3440644
  97.7 521.6 %copy-start.6 = (f32[64]{0:T(128)S(1)}, f32[64]{0:T(128)}, u32[]{:S(2)}) copy-start(f32[64]{0:T(128)} %param.14) | copy-start | bytes 772
  97.7 521.7 %copy-start.7 = (s32[8]{0:T(128)S(1)}, s32[8]{0:T(128)}, u32[]{:S(2)}) copy-start(s32[8]{0:T(128)} %param.19) | copy-start | bytes 100
  97.7 304.5 %collective-permute-start.2 = (bf16[2,4,224,640]{3,2,1,0:T(8,128)(2,1)S(1)}, bf16[2,4,224,640]{3,2,1,0:T(8,128)(2,1)S(1)}, u32[]{:S(2)}, u32[]{:S(2)}) collective-permute-start(bf16[2,4,224,640]{3,2,1,0:T(8,128)(2,1)S(1)} %pad_maximum_fusion.1), channel_id=1, source_target_pairs={{0,16},{4,20},{8,24},{12,28},{16,0},{20,4},{24,8},{28,12},{32,48},... | collective-permute-start | bytes 6881288 | tf_op jit(solution)/shard_map/ppermute | solution.py:16
  402.2 3.5 copy-start.4
  405.7 407.9 %collective-permute-start.3 = (bf16[2,8,224,640]{3,2,1,0:T(8,128)(2,1)}, bf16[2,8,224,640]{3,2,1,0:T(8,128)(2,1)}, u32[]{:S(2)}, u32[]{:S(2)}) collective-permute-start(bf16[2,8,224,640]{3,2,1,0:T(8,128)(2,1)} %pad_maximum_fusion), channel_id=1, source_target_pairs={{0,32},{4,36},{8,40},{12,44},{16,48},{20,52},{24,56},{28,60},{32,0... | collective-permute-start | bytes 13762568 | tf_op jit(solution)/shard_map/ppermute | solution.py:16
  620.9 4.0 copy-start.2
  620.9 5.2 copy-start.5
Sparse Core Ops, SparseCore 0:
  910.0 43.5 reduce-scatter.3
where the time goes:
time: 965 us; the launch traced here: 963 us
  waiting for transfers between devices  583 us (60%)
  starting transfers between devices  233 us (24%)
  matrix products  52.3 us (5%)
  local copies, waits for them, and re-layouts  43.2 us (4%)
  other arithmetic  31.9 us (3%)
  between operations  13.6 us (1%)
    ppermute x4, waiting for transfers between devices, from_partner(): return lax.ppermute(value, axis, pairs)  540 us
    ppermute x4, starting transfers between devices, from_partner(): return lax.ppermute(value, axis, pairs)  233 us
    unnamed x2, waiting for transfers between devices  43 us
    dot_general x10, matrix products, one_head(): return jnp.dot(weights, value_head, preferred_element_type=jnp.float32)  29.4 us
    dot_general x10, matrix products, one_head(): lax.dot_general(query_head, key_head, (((1,), (1,)), ((), ())), preferred...  20.9 us
  transfers between devices with their start and end apart: 5, of which 5 were waited for; matrix products, arithmetic and copies ran while one was open for 1% of the time, Pallas kernels for 0%

commit v1 on v0

v1 whole, which is shorter than its diff:
```python
import jax
import jax.numpy as jnp
from jax import lax
from jax.experimental import pallas as pl
from jax.experimental.pallas import tpu as pltpu
from jax.sharding import PartitionSpec as P

HEADS = 38
HEAD_DIM = 64
RING = 16
SLOTS = 10
IMG = 192
KEYS = 224
HALF = IMG // 2
PAIR = 2 * HEAD_DIM
CHUNK = 4 * IMG
STEP = 2 * KEYS
LOG2E = 1.4426950408889634
MESH = pl.DeviceIdType.MESH
epsilon = 1e-06


def lanes(shape):
    return lax.broadcasted_iota(jnp.int32, shape, 1)


def pack(low, high):
    first = lanes(low.shape) < HEAD_DIM
    even = jnp.where(first, low, pltpu.roll(high, HEAD_DIM, 1))
    odd = jnp.where(first, pltpu.roll(low, HEAD_DIM, 1), high)
    return even.astype(jnp.bfloat16), odd.astype(jnp.bfloat16)


def normed(value, gain, ones):
    x = value.astype(jnp.float32)
    square = x * x
    high = square.astype(jnp.bfloat16)
    low = (square - high.astype(jnp.float32)).astype(jnp.bfloat16)
    total = jnp.dot(high, ones, preferred_element_type=jnp.float32)
    total += jnp.dot(low, ones, preferred_element_type=jnp.float32)
    inverse = lax.rsqrt(total * (1.0 / HEAD_DIM) + epsilon)
    return (x * inverse * gain).astype(jnp.bfloat16).astype(jnp.float32)


def prep_kernel(count_ref, q_ref, k_ref, v_ref, qg_ref, kg_ref, qp_ref, kvp_ref):
    pos = lax.axis_index("seq")
    rank = lax.rem(pos, RING)
    left = count_ref[lax.div(pos, RING)] - rank * IMG
    row = lax.broadcasted_iota(jnp.int32, (PAIR, PAIR), 0) < HEAD_DIM
    column = lanes((PAIR, PAIR)) < HEAD_DIM
    ones = jnp.where(row == column, 1.0, 0.0).astype(jnp.bfloat16)
    q_gain = jnp.concatenate([qg_ref[...], qg_ref[...]], axis=1)
    k_gain = jnp.concatenate([kg_ref[...], kg_ref[...]], axis=1)
    key_row = lax.broadcasted_iota(jnp.int32, (KEYS, PAIR), 0)
    gain_rows = jnp.where(key_row < IMG, k_gain[0:1], k_gain[1:2])
    dead = (key_row < IMG) & (key_row >= left)
    for p in range(SLOTS // 2):
        columns = slice(p * PAIR, (p + 1) * PAIR)
        q = normed(q_ref[:, columns], q_gain, ones) * HEAD_DIM ** (-0.5)
        qp_ref[2 * p], qp_ref[2 * p + 1] = pack(q[:HALF], q[HALF:])
        k = normed(k_ref[:, columns], gain_rows, ones)
        k = jnp.where(dead, k[IMG : IMG + 1], k)
        v = jnp.where(dead, 0.0, v_ref[:, columns].astype(jnp.float32))
        kvp_ref[2 * p], kvp_ref[2 * p + 1] = pack(k, v)


def near(i):
    return RING + (2 * lax.rem(i, 2) - 1) * lax.div(i + 1, 2)


def role(z, core):
    part, quarter = lax.rem(z, 4), lax.div(z, 4)
    double = lax.div(4 - part, 4)
    odd = lax.rem(part, 2)
    middle = (1 - double) * (1 - odd)
    owner = double * core + odd * lax.div(part, 2) + middle * lax.rem(quarter, 2)
    slot = double * quarter + odd * (4 + quarter) + middle * (8 + lax.div(z, 8))
    return double, owner, slot


def main_kernel(
    count_ref, qp_ref, kvp_ref, att_ref,
    kv_buf, q_buf, q_all, m_all, acc_all, o_stage, o_buf,
    kv_send, kv_recv, q_send, q_recv, o_send, o_recv, relay_send,
):
    pos = lax.axis_index("seq")
    tp = lax.axis_index("tp")
    z = lax.rem(pos, RING)
    base = pos - z
    core = lax.rem(tp, 2)
    tp_base = tp - core
    double, owner, my_slot = role(z, core)
    parity = lax.rem(z, 2)

    barrier = pltpu.get_barrier_semaphore()
    linear = z * 2 + core

    def greet(i, _):
        peer = lax.rem(linear + i, 2 * RING)
        pl.semaphore_signal(
            barrier,
            inc=1,
            device_id=(base + lax.div(peer, 2), tp_base + lax.rem(peer, 2)),
            device_id_type=MESH,
        )
        return 0

    lax.fori_loop(1, 2 * RING, greet, 0)
    pl.semaphore_wait(barrier, 2 * RING - 1)

    def target(i):
        chip = lax.rem(z + 2 * RING - near(i), RING)
        return (chip,) + role(chip, core)

    def q_copy(i):
        chip, dbl, _, slot = target(i)
        to_core = dbl * core + (1 - dbl) * parity
        place = dbl * z + (1 - dbl) * lax.div(z, 2)
        return pltpu.make_async_remote_copy(
            src_ref=qp_ref.at[slot], dst_ref=q_buf.at[place],
            send_sem=q_send.at[i], recv_sem=q_recv.at[place],
            device_id=(base + chip, tp_base + to_core), device_id_type=MESH,
        )

    q_local = double * z + (1 - double) * lax.div(z, 2)
    q_stays = (owner == core) & ((double == 1) | (parity == core))

    def q_start(k, _):
        i = RING - 1 - k

        @pl.when(target(i)[2] == core)
        def _():
            q_copy(i).start()

        return 0

    lax.fori_loop(0, RING - 1, q_start, 0)

    @pl.when(q_stays)
    def _():
        pltpu.make_async_copy(qp_ref.at[my_slot], q_buf.at[q_local], q_recv.at[q_local]).start()

    @pl.when((owner == core) & jnp.logical_not(q_stays))
    def _():
        q_copy(0).start()

    def kv_copy(i):
        chip, _, _, slot = target(i)
        return pltpu.make_async_remote_copy(
            src_ref=kvp_ref.at[slot], dst_ref=kv_buf.at[i],
            send_sem=kv_send.at[i], recv_sem=kv_recv.at[i],
            device_id=(base + chip, tp), device_id_type=MESH,
        )

    @pl.when(owner == core)
    def _():
        pltpu.make_async_copy(kvp_ref.at[my_slot], kv_buf.at[0], kv_recv.at[0]).start()

    def kv_start(i, _):
        @pl.when(target(i)[2] == core)
        def _():
            kv_copy(i).start()

        return 0

    lax.fori_loop(1, RING, kv_start, 0)

    def relay(i):
        return pltpu.make_async_remote_copy(
            src_ref=kv_buf.at[i], dst_ref=kv_buf.at[i],
            send_sem=relay_send.at[i], recv_sem=kv_recv.at[i],
            device_id=(pos, tp_base + 1 - core), device_id_type=MESH,
        )

    relays = (double == 0) & (owner == core)

    places = 8 + 8 * double
    chunks = 2 + 2 * double

    def unpack(s, _):
        pltpu.make_async_copy(q_buf.at[s], q_buf.at[s], q_recv.at[s]).wait()
        packed = q_buf[s].astype(jnp.float32)
        first = lanes((HALF, PAIR)) < HEAD_DIM
        q_all[s, :HALF] = jnp.where(first, packed, 0.0).astype(jnp.bfloat16)
        q_all[s, HALF:] = jnp.where(first, pltpu.roll(packed, HEAD_DIM, 1), 0.0).astype(jnp.bfloat16)
        return 0

    lax.fori_loop(0, places, unpack, 0)
    m_all[...] = jnp.full_like(m_all, -jnp.inf)
    acc_all[...] = jnp.zeros_like(acc_all)
    count = count_ref[lax.div(pos, RING)]

    def key_step(i, _):
        for n in range(2):
            slot = 2 * i + n
            pltpu.make_async_copy(kv_buf.at[slot], kv_buf.at[slot], kv_recv.at[slot]).wait()

            @pl.when(relays)
            def _():
                relay(slot).start()

        kv = kv_buf[pl.ds(2 * i, 2)].reshape(STEP, PAIR)
        lane = lanes((16, STEP))
        second = lane >= KEYS
        within = jnp.where(second, lane - KEYS, lane)
        rank = jnp.where(second, lax.rem(z + near(2 * i + 1), RING), lax.rem(z + near(2 * i), RING))
        live = (within >= IMG) | (rank * IMG + within < count)
        live = jnp.where(live, 1.0, 0.0).astype(jnp.bfloat16)
        value = jnp.concatenate([kv.T[HEAD_DIM:], live], axis=0)

        def chunk_step(j, _):
            q = q_all[pl.ds(4 * j, 4)].reshape(CHUNK, PAIR)
            s = lax.dot_general(
                kv, q, (((1,), (1,)), ((), ())), preferred_element_type=jnp.float32
            )
            m_old = m_all[j]
            m_new = jnp.maximum(m_old, jnp.max(s, axis=0, keepdims=True))
            p = jnp.exp2((s - m_new) * LOG2E).astype(jnp.bfloat16)
            decay = jnp.exp2((m_old - m_new) * LOG2E)
            acc_all[j] = acc_all[j] * decay + jnp.dot(value, p, preferred_element_type=jnp.float32)
            m_all[j] = m_new
            return 0

        lax.fori_loop(0, chunks, chunk_step, 0)
        return 0

    lax.fori_loop(0, RING // 2, key_step, 0)

    def home(s):
        return double * s + (1 - double) * (2 * s + core)

    def o_copy(s):
        return pltpu.make_async_remote_copy(
            src_ref=o_stage.at[s], dst_ref=o_buf.at[my_slot],
            send_sem=o_send.at[s], recv_sem=o_recv.at[my_slot],
            device_id=(base + home(s), tp_base + owner), device_id_type=MESH,
        )

    def stays(s):
        return (home(s) == z) & (owner == core)

    def finish(j, _):
        out = (acc_all[j, :HEAD_DIM] / acc_all[j, HEAD_DIM : HEAD_DIM + 1]).T
        for b in range(4):
            block = out[b * IMG : (b + 1) * IMG]
            both = jnp.concatenate([block[:HALF], block[HALF:]], axis=1)
            o_stage[4 * j + b] = both.astype(jnp.bfloat16)
        for b in range(4):
            s = 4 * j + b

            @pl.when(stays(s))
            def _():
                pltpu.make_async_copy(o_stage.at[s], o_buf.at[my_slot], o_recv.at[my_slot]).start()

            @pl.when(jnp.logical_not(stays(s)))
            def _():
                o_copy(s).start()

        return 0

    lax.fori_loop(0, chunks, finish, 0)

    limit = lax.div(HEADS + 3 - tp, 4)
    for j in range(SLOTS):
        pltpu.make_async_copy(o_buf.at[j], o_buf.at[j], o_recv.at[j]).wait()
        valid = jnp.where(j < limit, 1.0, 0.0)
        got = (o_buf[j].astype(jnp.float32) * valid).astype(jnp.bfloat16)
        columns = slice(j * HEAD_DIM, (j + 1) * HEAD_DIM)
        att_ref[:HALF, columns] = got[:, :HEAD_DIM]
        att_ref[HALF:, columns] = got[:, HEAD_DIM:]

    def drain(i, _):
        @pl.when(target(i)[2] == core)
        def _():
            q_copy(i).wait_send()
            kv_copy(i).wait_send()

        return 0

    lax.fori_loop(1, RING, drain, 0)

    @pl.when((owner == core) & jnp.logical_not(q_stays))
    def _():
        q_copy(0).wait_send()

    @pl.when(relays)
    def _():
        def relay_drain(i, _):
            relay(i).wait_send()
            return 0

        lax.fori_loop(0, RING, relay_drain, 0)

    def o_drain(s, _):
        @pl.when(jnp.logical_not(stays(s)))
        def _():
            o_copy(s).wait_send()

        return 0

    lax.fori_loop(0, places, o_drain, 0)


VMEM = pl.BlockSpec(memory_space=pltpu.VMEM)
SMEM = pl.BlockSpec(memory_space=pltpu.SMEM)


def local(query, keys, values, q_gain, k_gain, residual, gate, out_weight, image_count):
    bf16, f32 = jnp.bfloat16, jnp.float32
    q_packed, kv_packed = pl.pallas_call(
        prep_kernel,
        out_shape=(
            jax.ShapeDtypeStruct((SLOTS, HALF, PAIR), bf16),
            jax.ShapeDtypeStruct((SLOTS, KEYS, PAIR), bf16),
        ),
        in_specs=[SMEM] + [VMEM] * 5,
        out_specs=(VMEM, VMEM),
        name="prep",
    )(image_count, query, keys, values, q_gain.reshape(1, HEAD_DIM), k_gain)
    sem = pltpu.SemaphoreType.DMA
    attended = pl.pallas_call(
        main_kernel,
        out_shape=jax.ShapeDtypeStruct((IMG, SLOTS * HEAD_DIM), bf16),
        in_specs=[SMEM, VMEM, VMEM],
        out_specs=VMEM,
        scratch_shapes=[
            pltpu.VMEM((RING, KEYS, PAIR), bf16),
            pltpu.VMEM((RING, HALF, PAIR), bf16),
            pltpu.VMEM((RING, IMG, PAIR), bf16),
            pltpu.VMEM((4, 1, CHUNK), f32),
            pltpu.VMEM((4, HEAD_DIM + 16, CHUNK), f32),
            pltpu.VMEM((RING, HALF, PAIR), bf16),
            pltpu.VMEM((SLOTS, HALF, PAIR), bf16),
            sem((RING,)), sem((RING,)), sem((RING,)), sem((RING,)),
            sem((RING,)), sem((SLOTS,)), sem((RING,)),
        ],
        compiler_params=pltpu.CompilerParams(
            collective_id=0, has_side_effects=True, vmem_limit_bytes=48 * 2**20
        ),
        name="attend",
    )(image_count, q_packed, kv_packed)
    request = lax.axis_index("seq") // RING
    share = lax.psum_scatter(
        lax.dot_general(
            out_weight, attended, (((0,), (1,)), ((), ())), preferred_element_type=f32
        ).astype(bf16),
        "tp",
        scatter_dimension=0,
        tiled=True,
    ).astype(f32)
    projected = jnp.transpose(share)
    gate_row = lax.dynamic_index_in_dim(gate, request, 0, keepdims=False).astype(f32)
    return (residual.astype(f32) + gate_row[None, :] * projected).astype(bf16)


def solution(mesh):
    placed = (
        P("seq", "tp"),
        P("seq", "tp"),
        P("seq", "tp"),
        P(),
        P(),
        P("seq", "tp"),
        P(None, "tp"),
        P("tp", None),
        P(),
    )
    return jax.shard_map(
        local, mesh=mesh, in_specs=placed, out_specs=P("seq", "tp"), check_vma=False
    )
```

time: 965 us -> 153 us (0.16)
  waiting for transfers between devices: 583 us -> 48.8 us
  starting transfers between devices: 233 us -> 0.01 us
  Pallas kernels: 0 us -> 80.1 us
  matrix products: 52.3 us -> 1.9 us
  local copies, waits for them, and re-layouts: 43.2 us -> 6.16 us
  other arithmetic: 31.9 us -> 2.44 us
    ppermute x4 -> x0, waiting for transfers between devices: 540 us -> none  [from_partner(): return lax.ppermute(value, axis, pairs)]
    ppermute x4 -> x0, starting transfers between devices: 233 us -> none  [from_partner(): return lax.ppermute(value, axis, pairs)]
    pallas_call x0 -> x2, Pallas kernels: none -> 80.1 us  [the longest x1 77.1 us: local(): pl.pallas_call(main_kernel, out_shape=jax.ShapeDtypeStruct((IMG, SLOTS *...]
    dot_general x20 -> x0, matrix products: 50.3 us -> none  [the longest x10 29.4 us: one_head(): return jnp.dot(weights, value_head, preferred_element_type=jnp.float32)]
  transfers between devices with their start and end apart: 5 -> 1, of which waited for: 5 -> 1; matrix products, arithmetic and copies ran while one was open for 1% -> 0% of each run, Pallas kernels for 0% -> 0%
where the time goes in v1:
time: 153 us
  Pallas kernels  80.1 us (52%)
  waiting for transfers between devices  48.8 us (32%)
  between operations  13.4 us (9%)
  local copies, waits for them, and re-layouts  6.16 us (4%)
  other arithmetic  2.44 us (2%)
  matrix products  1.9 us (1%)
    pallas_call x1, Pallas kernels, local(): pl.pallas_call(main_kernel, out_shape=jax.ShapeDtypeStruct((IMG, SLOTS *...  77.1 us
    unnamed x2, waiting for transfers between devices  48.8 us
    unnamed x10, local copies, waits for them, and re-layouts  6.16 us
  transfers between devices with their start and end apart: 1, of which 1 were waited for; matrix products, arithmetic and copies ran while one was open for 0% of the time, Pallas kernels for 0%

profile of v1, /device:TPU:1, one launch (start us, length us, event | category | flops | bytes accessed | tf_op | source)
XLA Modules:
  0.0 152.8 jit_solution(2154494267624815084)
XLA Ops:
  6.5 0.0 copy-start
  6.5 0.0 reduce-scatter.4.cloned.1.call-start
  6.5 2.9 %prep.1 = (bf16[10,96,128]{2,1,0:T(8,128)(2,1)}, bf16[10,224,128]{2,1,0:T(8,128)(2,1)}) custom-call(s32[8]{0:T(128)} %count_ref.3, bf16[192,640]{1,0:T(8,128)(2,1)} %q_ref.1, bf16[224,640]{1,0:T(8,128)(2,1)} %k_ref.1, bf16[224,640]{1,0:T(8,128)(2,1)} %v_ref.1, f32[1,64]{1,0:T(1,128)} %bitcast.10, f32[2,64]{1,0:T(2,128)} %kg_ref.1), custom_call_target="tpu_custom_call" | custom-call | tf_op jit(solution)/shard_map/prep/pallas_call | solution.py:310
  9.5 0.0 copy-start.1
  9.5 1.1 copy-done.1
  10.5 0.0 copy-start.2
  10.5 0.9 copy-done.2
  11.5 0.0 copy-start.3
  11.5 0.7 copy-done.3
  12.1 77.1 %attend.1 = bf16[192,640]{1,0:T(8,128)(2,1)S(1)} custom-call(s32[8]{0:T(128)S(1)} %copy-done.3, bf16[10,96,128]{2,1,0:T(8,128)(2,1)S(1)} %copy-done.2, bf16[10,224,128]{2,1,0:T(8,128)(2,1)S(1)} %copy-done.1), custom_call_target="tpu_custom_call" | custom-call | tf_op jit(solution)/shard_map/attend/pallas_call | solution.py:321
  89.3 0.0 copy-done
  89.3 1.9 %fusion = bf16[2432,192]{0,1:T(8,128)(2,1)} fusion(bf16[192,640]{1,0:T(8,128)(2,1)S(1)} %attend.1, bf16[640,2432]{1,0:T(8,128)(2,1)S(1)} %copy-done), kind=kOutput, calls=%fused_computation.1 | convolution fusion | flops 598155264 | bytes 4292608 | tf_op jit(solution)/shard_map/dot_general | solution.py:344
  91.2 2.4 %copy.10 = bf16[2432,192]{1,0:T(8,128)(2,1)} copy(bf16[2432,192]{0,1:T(8,128)(2,1)} %fusion) | data formatting | bytes 1867776
  93.6 0.0 reduce-scatter.4.cloned.1.call-update
  93.6 0.7 convert_reduce_fusion
  94.3 48.8 %reduce-scatter.4.cloned.1.call-done = bf16[608,192]{1,0:T(8,128)(2,1)} async-done(((bf16[2432,192]{1,0:T(8,128)(2,1)}), bf16[608,192]{1,0:T(8,128)(2,1)}) %reduce-scatter.4.cloned.1.call-update) | async-done | bytes 233488
  143.1 1.1 copy.11
  144.3 1.7 %fusion.1 = bf16[192,608]{1,0:T(8,128)(2,1)} fusion(bf16[608,192]{0,1:T(8,128)(2,1)S(1)} %copy.11, bf16[192,608]{1,0:T(8,128)(2,1)} %param.14, f32[608]{0:T(1024)S(1)} %convert_reduce_fusion), kind=kLoop, calls=%fused_computation.3 | loop fusion | flops 583680 | bytes 702848 | tf_op jit(solution)/shard_map/convert_element_type | solution.py:353
Async XLA Ops:
  6.5 82.8 %copy-start = (bf16[640,2432]{1,0:T(8,128)(2,1)S(1)}, bf16[640,2432]{1,0:T(8,128)(2,1)}, u32[]{:S(2)}) copy-start(bf16[640,2432]{1,0:T(8,128)(2,1)} %param.16) | copy-start | bytes 9338884
  6.5 136.6 %reduce-scatter.4.cloned.1.call-start = ((), (), s32[]{:S(2)}) async-start(), calls=%async_computation.1 | async-start | bytes 1556480
  9.5 1.1 copy-start.1
  10.5 0.9 copy-start.2
  11.5 0.7 copy-start.3
Sparse Core Ops, SparseCore 0:
  93.7 49.3 reduce-scatter.3

commit v2 on v1

--- a/solution.py
+++ b/solution.py
@@ -15,6 +15,9 @@
 PAIR = 2 * HEAD_DIM
 CHUNK = 4 * IMG
 STEP = 2 * KEYS
+WIDE = 608
+BLOCKS = 2
+ROWS = IMG // BLOCKS
 LOG2E = 1.4426950408889634
 MESH = pl.DeviceIdType.MESH
 epsilon = 1e-06
@@ -42,22 +45,28 @@
     return (x * inverse * gain).astype(jnp.bfloat16).astype(jnp.float32)
 
 
-def prep_kernel(count_ref, q_ref, k_ref, v_ref, qg_ref, kg_ref, qp_ref, kvp_ref):
-    pos = lax.axis_index("seq")
-    rank = lax.rem(pos, RING)
-    left = count_ref[lax.div(pos, RING)] - rank * IMG
+def ones_pair():
     row = lax.broadcasted_iota(jnp.int32, (PAIR, PAIR), 0) < HEAD_DIM
     column = lanes((PAIR, PAIR)) < HEAD_DIM
-    ones = jnp.where(row == column, 1.0, 0.0).astype(jnp.bfloat16)
-    q_gain = jnp.concatenate([qg_ref[...], qg_ref[...]], axis=1)
-    k_gain = jnp.concatenate([kg_ref[...], kg_ref[...]], axis=1)
+    return jnp.where(row == column, 1.0, 0.0).astype(jnp.bfloat16)
+
+
+def pack_queries(q_ref, qg_ref, qp_ref):
+    gain = jnp.concatenate([qg_ref[...], qg_ref[...]], axis=1)
+    ones = ones_pair()
+    for p in range(SLOTS // 2):
+        q = normed(q_ref[:, p * PAIR : (p + 1) * PAIR], gain, ones) * HEAD_DIM ** (-0.5)
+        qp_ref[2 * p], qp_ref[2 * p + 1] = pack(q[:HALF], q[HALF:])
+
+
+def pack_keys(left, k_ref, v_ref, kg_ref, kvp_ref):
+    gain = jnp.concatenate([kg_ref[...], kg_ref[...]], axis=1)
+    ones = ones_pair()
     key_row = lax.broadcasted_iota(jnp.int32, (KEYS, PAIR), 0)
-    gain_rows = jnp.where(key_row < IMG, k_gain[0:1], k_gain[1:2])
+    gain_rows = jnp.where(key_row < IMG, gain[0:1], gain[1:2])
     dead = (key_row < IMG) & (key_row >= left)
     for p in range(SLOTS // 2):
         columns = slice(p * PAIR, (p + 1) * PAIR)
-        q = normed(q_ref[:, columns], q_gain, ones) * HEAD_DIM ** (-0.5)
-        qp_ref[2 * p], qp_ref[2 * p + 1] = pack(q[:HALF], q[HALF:])
         k = normed(k_ref[:, columns], gain_rows, ones)
         k = jnp.where(dead, k[IMG : IMG + 1], k)
         v = jnp.where(dead, 0.0, v_ref[:, columns].astype(jnp.float32))
@@ -79,9 +88,12 @@
 
 
 def main_kernel(
-    count_ref, qp_ref, kvp_ref, att_ref,
-    kv_buf, q_buf, q_all, m_all, acc_all, o_stage, o_buf,
+    count_ref, q_hbm, k_hbm, v_hbm, qg_ref, kg_ref, res_hbm, gate_ref, w_hbm, out_ref,
+    q_in, k_in, v_in, res_in, w_in, qp_ref, kvp_ref,
+    kv_buf, q_buf, q_all, m_all, acc_all, o_stage, o_buf, att_ref,
+    part, pair_in, mate_out, mate_in, load,
     kv_send, kv_recv, q_send, q_recv, o_send, o_recv, relay_send,
+    pair_send, pair_recv, mate_send, mate_recv,
 ):
     pos = lax.axis_index("seq")
     tp = lax.axis_index("tp")
@@ -91,6 +103,18 @@
     tp_base = tp - core
     double, owner, my_slot = role(z, core)
     parity = lax.rem(z, 2)
+    side = lax.div(tp, 2)
+    mate = (pos, 2 * (1 - side) + core)
+    sibling = (pos, tp_base + 1 - core)
+
+    loads = [
+        pltpu.make_async_copy(source, place, load.at[n])
+        for n, (source, place) in enumerate(
+            [(q_hbm, q_in), (k_hbm, k_in), (v_hbm, v_in), (res_hbm, res_in), (w_hbm, w_in)]
+        )
+    ]
+    for copy in loads:
+        copy.start()
 
     barrier = pltpu.get_barrier_semaphore()
     linear = z * 2 + core
@@ -106,7 +130,14 @@
         return 0
 
     lax.fori_loop(1, 2 * RING, greet, 0)
-    pl.semaphore_wait(barrier, 2 * RING - 1)
+    pl.semaphore_signal(barrier, inc=1, device_id=mate, device_id_type=MESH)
+    count = count_ref[lax.div(pos, RING)]
+    loads[0].wait()
+    pack_queries(q_in, qg_ref, qp_ref)
+    loads[1].wait()
+    loads[2].wait()
+    pack_keys(count - z * IMG, k_in, v_in, kg_ref, kvp_ref)
+    pl.semaphore_wait(barrier, 2 * RING)
 
     def target(i):
         chip = lax.rem(z + 2 * RING - near(i), RING)
@@ -169,7 +200,7 @@
         return pltpu.make_async_remote_copy(
             src_ref=kv_buf.at[i], dst_ref=kv_buf.at[i],
             send_sem=relay_send.at[i], recv_sem=kv_recv.at[i],
-            device_id=(pos, tp_base + 1 - core), device_id_type=MESH,
+            device_id=sibling, device_id_type=MESH,
         )
 
     relays = (double == 0) & (owner == core)
@@ -188,7 +219,6 @@
     lax.fori_loop(0, places, unpack, 0)
     m_all[...] = jnp.full_like(m_all, -jnp.inf)
     acc_all[...] = jnp.zeros_like(acc_all)
-    count = count_ref[lax.div(pos, RING)]
 
     def key_step(i, _):
         for n in range(2):
@@ -269,6 +299,48 @@
         att_ref[:HALF, columns] = got[:, :HEAD_DIM]
         att_ref[HALF:, columns] = got[:, HEAD_DIM:]
 
+    def pair_copy(n):
+        return pltpu.make_async_remote_copy(
+            src_ref=part.at[n, 1 - core], dst_ref=pair_in.at[n],
+            send_sem=pair_send.at[n], recv_sem=pair_recv.at[n],
+            device_id=sibling, device_id_type=MESH,
+        )
+
+    def mate_copy(n):
+        return pltpu.make_async_remote_copy(
+            src_ref=mate_out.at[n], dst_ref=mate_in.at[n],
+            send_sem=mate_send.at[n], recv_sem=mate_recv.at[n],
+            device_id=mate, device_id_type=MESH,
+        )
+
+    loads[4].wait()
+    for n in range(BLOCKS):
+        product = jnp.dot(
+            att_ref[n * ROWS : (n + 1) * ROWS], w_in[...], preferred_element_type=jnp.float32
+        ).astype(jnp.bfloat16)
+        for t in range(4):
+            part[n, t % 2, t // 2] = product[:, t * WIDE : (t + 1) * WIDE]
+        pair_copy(n).start()
+    for n in range(BLOCKS):
+        pair_copy(n).wait_recv()
+        both = part[n, core, 1 - side].astype(jnp.float32) + pair_in[n, 1 - side].astype(jnp.float32)
+        mate_out[n] = both.astype(jnp.bfloat16)
+        mate_copy(n).start()
+    loads[3].wait()
+    gates = gate_ref[...].astype(jnp.float32)
+    chosen = lax.broadcasted_iota(jnp.int32, gates.shape, 0) == lax.div(pos, RING)
+    gate_row = jnp.sum(jnp.where(chosen, gates, 0.0), axis=0, keepdims=True)
+    for n in range(BLOCKS):
+        rows = slice(n * ROWS, (n + 1) * ROWS)
+        both = part[n, core, side].astype(jnp.float32) + pair_in[n, side].astype(jnp.float32)
+        mate_copy(n).wait_recv()
+        projected = both + mate_in[n].astype(jnp.float32)
+        updated = res_in[rows].astype(jnp.float32) + gate_row * projected
+        out_ref[rows] = updated.astype(jnp.bfloat16)
+    for n in range(BLOCKS):
+        pair_copy(n).wait_send()
+        mate_copy(n).wait_send()
+
     def drain(i, _):
         @pl.when(target(i)[2] == core)
         def _():
@@ -303,27 +375,25 @@
 
 VMEM = pl.BlockSpec(memory_space=pltpu.VMEM)
 SMEM = pl.BlockSpec(memory_space=pltpu.SMEM)
+HBM = pl.BlockSpec(memory_space=pltpu.HBM)
 
 
 def local(query, keys, values, q_gain, k_gain, residual, gate, out_weight, image_count):
     bf16, f32 = jnp.bfloat16, jnp.float32
-    q_packed, kv_packed = pl.pallas_call(
-        prep_kernel,
-        out_shape=(
-            jax.ShapeDtypeStruct((SLOTS, HALF, PAIR), bf16),
-            jax.ShapeDtypeStruct((SLOTS, KEYS, PAIR), bf16),
-        ),
-        in_specs=[SMEM] + [VMEM] * 5,
-        out_specs=(VMEM, VMEM),
-        name="prep",
-    )(image_count, query, keys, values, q_gain.reshape(1, HEAD_DIM), k_gain)
     sem = pltpu.SemaphoreType.DMA
-    attended = pl.pallas_call(
+    return pl.pallas_call(
         main_kernel,
-        out_shape=jax.ShapeDtypeStruct((IMG, SLOTS * HEAD_DIM), bf16),
-        in_specs=[SMEM, VMEM, VMEM],
+        out_shape=jax.ShapeDtypeStruct(residual.shape, bf16),
+        in_specs=[SMEM, HBM, HBM, HBM, VMEM, VMEM, HBM, VMEM, HBM],
         out_specs=VMEM,
         scratch_shapes=[
+            pltpu.VMEM(query.shape, bf16),
+            pltpu.VMEM(keys.shape, bf16),
+            pltpu.VMEM(values.shape, bf16),
+            pltpu.VMEM(residual.shape, bf16),
+            pltpu.VMEM(out_weight.shape, bf16),
+            pltpu.VMEM((SLOTS, HALF, PAIR), bf16),
+            pltpu.VMEM((SLOTS, KEYS, PAIR), bf16),
             pltpu.VMEM((RING, KEYS, PAIR), bf16),
             pltpu.VMEM((RING, HALF, PAIR), bf16),
             pltpu.VMEM((RING, IMG, PAIR), bf16),
@@ -331,26 +401,24 @@
             pltpu.VMEM((4, HEAD_DIM + 16, CHUNK), f32),
             pltpu.VMEM((RING, HALF, PAIR), bf16),
             pltpu.VMEM((SLOTS, HALF, PAIR), bf16),
+            pltpu.VMEM((IMG, SLOTS * HEAD_DIM), bf16),
+            pltpu.VMEM((BLOCKS, 2, 2, ROWS, WIDE), bf16),
+            pltpu.VMEM((BLOCKS, 2, ROWS, WIDE), bf16),
+            pltpu.VMEM((BLOCKS, ROWS, WIDE), bf16),
+            pltpu.VMEM((BLOCKS, ROWS, WIDE), bf16),
+            sem((5,)),
             sem((RING,)), sem((RING,)), sem((RING,)), sem((RING,)),
             sem((RING,)), sem((SLOTS,)), sem((RING,)),
+            sem((BLOCKS,)), sem((BLOCKS,)), sem((BLOCKS,)), sem((BLOCKS,)),
         ],
         compiler_params=pltpu.CompilerParams(
-            collective_id=0, has_side_effects=True, vmem_limit_bytes=48 * 2**20
+            collective_id=0, has_side_effects=True, vmem_limit_bytes=65_000_000
         ),
         name="attend",
-    )(image_count, q_packed, kv_packed)
-    request = lax.axis_index("seq") // RING
-    share = lax.psum_scatter(
-        lax.dot_general(
-            out_weight, attended, (((0,), (1,)), ((), ())), preferred_element_type=f32
-        ).astype(bf16),
-        "tp",
-        scatter_dimension=0,
-        tiled=True,
-    ).astype(f32)
-    projected = jnp.transpose(share)
-    gate_row = lax.dynamic_index_in_dim(gate, request, 0, keepdims=False).astype(f32)
-    return (residual.astype(f32) + gate_row[None, :] * projected).astype(bf16)
+    )(
+        image_count, query, keys, values, q_gain.reshape(1, HEAD_DIM), k_gain,
+        residual, gate, out_weight,
+    )
 
 
 def solution(mesh):

time: 153 us -> 92.4 us (0.60)
  waiting for transfers between devices: 48.8 us -> 0 us
  between operations: 13.4 us -> 0.01 us
  Pallas kernels: 80.1 us -> 89.8 us
  local copies, waits for them, and re-layouts: 6.16 us -> 1.66 us
  other arithmetic: 2.44 us -> 0 us
  matrix products: 1.9 us -> 0 us
    unnamed x2 -> x0, waiting for transfers between devices: 48.8 us -> none
    pallas_call x2 -> x1, Pallas kernels: 80.1 us -> 89.8 us  [local(): pl.pallas_call(main_kernel, out_shape=jax.ShapeDtypeStruct(residual.shape...]
    unnamed x10 -> x1, local copies, waits for them, and re-layouts: 6.16 us -> 1.66 us
    dot_general x1 -> x0, matrix products: 1.9 us -> none  [local(): lax.dot_general(out_weight, attended, (((0,), (1,)), ((), ())), preferred...]
    convert_element_type x1 -> x0, other arithmetic: 1.72 us -> none  [local(): return (residual.astype(f32) + gate_row[None, :] * projected).astype(bf16)]
  transfers between devices with their start and end apart: 1 -> 0, of which waited for: 1 -> 0; matrix products, arithmetic and copies ran while one was open for 0% -> 0% of each run, Pallas kernels for 0% -> 0%
where the time goes in v2:
time: 92.4 us; the launch traced here: 91.5 us
  Pallas kernels  89.8 us (97%)
  local copies, waits for them, and re-layouts  1.66 us (2%)
    pallas_call x1, Pallas kernels, local(): pl.pallas_call(main_kernel, out_shape=jax.ShapeDtypeStruct(residual.shape...  89.8 us

profile of v2, /device:TPU:1, one launch (start us, length us, event | category | flops | bytes accessed | tf_op | source)
XLA Modules:
  0.0 91.5 jit_solution(11290942959637239190)
XLA Ops:
  0.0 89.8 %attend.1 = bf16[192,608]{1,0:T(8,128)(2,1)} custom-call(s32[8]{0:T(128)} %count_ref.1, bf16[192,640]{1,0:T(8,128)(2,1)} %q_hbm.1, bf16[224,640]{1,0:T(8,128)(2,1)} %k_hbm.1, bf16[224,640]{1,0:T(8,128)(2,1)} %v_hbm.1, f32[1,64]{1,0:T(1,128)} %bitcast.1, f32[2,64]{1,0:T(2,128)} %kg_ref.1, bf16[192,608]{1,0:T(8,128)(2,1)} %res_hbm.1, bf16[8,608]{1,0:T(8,128)(2,1)} %gate_ref.1, ...), custom_call_target="tpu_custom_call" | custom-call | tf_op jit(solution)/shard_map/attend/pallas_call | solution.py:384
  89.8 1.7 %copy.11 = bf16[192,608]{1,0:T(8,128)(2,1)} copy(bf16[192,608]{1,0:T(8,128)(2,1)} %attend.1) | data formatting | bytes 466944

commit v3 on v2

--- a/solution.py
+++ b/solution.py
@@ -13,10 +13,11 @@
 KEYS = 224
 HALF = IMG // 2
 PAIR = 2 * HEAD_DIM
-CHUNK = 4 * IMG
+GROUP = 8
+CHUNK = GROUP * IMG
 STEP = 2 * KEYS
 WIDE = 608
-BLOCKS = 2
+BLOCKS = 4
 ROWS = IMG // BLOCKS
 LOG2E = 1.4426950408889634
 MESH = pl.DeviceIdType.MESH
@@ -102,7 +103,6 @@
     core = lax.rem(tp, 2)
     tp_base = tp - core
     double, owner, my_slot = role(z, core)
-    parity = lax.rem(z, 2)
     side = lax.div(tp, 2)
     mate = (pos, 2 * (1 - side) + core)
     sibling = (pos, tp_base + 1 - core)
@@ -134,46 +134,61 @@
     count = count_ref[lax.div(pos, RING)]
     loads[0].wait()
     pack_queries(q_in, qg_ref, qp_ref)
+    pl.semaphore_wait(barrier, 2 * RING)
+
+    def target(i):
+        chip = lax.rem(z + 2 * RING - near(i), RING)
+        return (chip,) + role(chip, core)
+
+    def q_copy(i):
+        chip, dbl, _, slot = target(i)
+        to_core = dbl * core + (1 - dbl) * lax.rem(lax.div(i, 2), 2)
+        place = dbl * i + (1 - dbl) * (2 * lax.div(i, 4) + lax.rem(i, 2))
+        return pltpu.make_async_remote_copy(
+            src_ref=qp_ref.at[slot], dst_ref=q_buf.at[place],
+            send_sem=q_send.at[i], recv_sem=q_recv.at[place],
+            device_id=(base + chip, tp_base + to_core), device_id_type=MESH,
+        )
+
+    q_stays = (owner == core) & ((double == 1) | (core == 0))
+
+    def q_pass(kind):
+        def q_start(k, _):
+            i = RING - 1 - k
+            _, dbl, own, _ = target(i)
+
+            @pl.when((own == core) & (dbl == kind))
+            def _():
+                q_copy(i).start()
+
+            return 0
+
+        lax.fori_loop(0, RING - 1, q_start, 0)
+
+    def kv_pass(kind):
+        def kv_start(i, _):
+            _, dbl, own, _ = target(i)
+
+            @pl.when((own == core) & (dbl == kind))
+            def _():
+                kv_copy(i).start()
+
+            return 0
+
+        lax.fori_loop(1, RING, kv_start, 0)
+
+    q_pass(1)
+    @pl.when(q_stays)
+    def _():
+        pltpu.make_async_copy(qp_ref.at[my_slot], q_buf.at[0], q_recv.at[0]).start()
+
+    @pl.when((owner == core) & jnp.logical_not(q_stays))
+    def _():
+        q_copy(0).start()
+
     loads[1].wait()
     loads[2].wait()
     pack_keys(count - z * IMG, k_in, v_in, kg_ref, kvp_ref)
-    pl.semaphore_wait(barrier, 2 * RING)
-
-    def target(i):
-        chip = lax.rem(z + 2 * RING - near(i), RING)
-        return (chip,) + role(chip, core)
-
-    def q_copy(i):
-        chip, dbl, _, slot = target(i)
-        to_core = dbl * core + (1 - dbl) * parity
-        place = dbl * z + (1 - dbl) * lax.div(z, 2)
-        return pltpu.make_async_remote_copy(
-            src_ref=qp_ref.at[slot], dst_ref=q_buf.at[place],
-            send_sem=q_send.at[i], recv_sem=q_recv.at[place],
-            device_id=(base + chip, tp_base + to_core), device_id_type=MESH,
-        )
-
-    q_local = double * z + (1 - double) * lax.div(z, 2)
-    q_stays = (owner == core) & ((double == 1) | (parity == core))
-
-    def q_start(k, _):
-        i = RING - 1 - k
-
-        @pl.when(target(i)[2] == core)
-        def _():
-            q_copy(i).start()
-
-        return 0
-
-    lax.fori_loop(0, RING - 1, q_start, 0)
-
-    @pl.when(q_stays)
-    def _():
-        pltpu.make_async_copy(qp_ref.at[my_slot], q_buf.at[q_local], q_recv.at[q_local]).start()
-
-    @pl.when((owner == core) & jnp.logical_not(q_stays))
-    def _():
-        q_copy(0).start()
 
     def kv_copy(i):
         chip, _, _, slot = target(i)
@@ -187,14 +202,9 @@
     def _():
         pltpu.make_async_copy(kvp_ref.at[my_slot], kv_buf.at[0], kv_recv.at[0]).start()
 
-    def kv_start(i, _):
-        @pl.when(target(i)[2] == core)
-        def _():
-            kv_copy(i).start()
-
-        return 0
-
-    lax.fori_loop(1, RING, kv_start, 0)
+    kv_pass(1)
+    q_pass(0)
+    kv_pass(0)
 
     def relay(i):
         return pltpu.make_async_remote_copy(
@@ -206,7 +216,7 @@
     relays = (double == 0) & (owner == core)
 
     places = 8 + 8 * double
-    chunks = 2 + 2 * double
+    chunks = 1 + double
 
     def unpack(s, _):
         pltpu.make_async_copy(q_buf.at[s], q_buf.at[s], q_recv.at[s]).wait()
@@ -220,7 +230,7 @@
     m_all[...] = jnp.full_like(m_all, -jnp.inf)
     acc_all[...] = jnp.zeros_like(acc_all)
 
-    def key_step(i, _):
+    def arrive(i):
         for n in range(2):
             slot = 2 * i + n
             pltpu.make_async_copy(kv_buf.at[slot], kv_buf.at[slot], kv_recv.at[slot]).wait()
@@ -238,66 +248,90 @@
         live = jnp.where(live, 1.0, 0.0).astype(jnp.bfloat16)
         value = jnp.concatenate([kv.T[HEAD_DIM:], live], axis=0)
 
-        def chunk_step(j, _):
-            q = q_all[pl.ds(4 * j, 4)].reshape(CHUNK, PAIR)
-            s = lax.dot_general(
-                kv, q, (((1,), (1,)), ((), ())), preferred_element_type=jnp.float32
-            )
-            m_old = m_all[j]
-            m_new = jnp.maximum(m_old, jnp.max(s, axis=0, keepdims=True))
-            p = jnp.exp2((s - m_new) * LOG2E).astype(jnp.bfloat16)
-            decay = jnp.exp2((m_old - m_new) * LOG2E)
-            acc_all[j] = acc_all[j] * decay + jnp.dot(value, p, preferred_element_type=jnp.float32)
-            m_all[j] = m_new
+        return kv, value
+
+    def chunk_step(kv, value, j):
+        q = q_all[pl.ds(GROUP * j, GROUP)].reshape(CHUNK, PAIR)
+        s = lax.dot_general(kv, q, (((1,), (1,)), ((), ())), preferred_element_type=jnp.float32)
+        m_old = m_all[j]
+        m_new = jnp.maximum(m_old, jnp.max(s, axis=0, keepdims=True))
+        p = jnp.exp2((s - m_new) * LOG2E).astype(jnp.bfloat16)
+        decay = jnp.exp2((m_old - m_new) * LOG2E)
+        acc_all[j] = acc_all[j] * decay + jnp.dot(value, p, preferred_element_type=jnp.float32)
+        m_all[j] = m_new
+
+    def key_step(i, _):
+        kv, value = arrive(i)
+
+        def each(j, _):
+            chunk_step(kv, value, j)
             return 0
 
-        lax.fori_loop(0, chunks, chunk_step, 0)
-        return 0
-
-    lax.fori_loop(0, RING // 2, key_step, 0)
+        lax.fori_loop(0, chunks, each, 0)
+        return 0
+
+    lax.fori_loop(0, RING // 2 - 1, key_step, 0)
 
     def home(s):
-        return double * s + (1 - double) * (2 * s + core)
-
-    def o_copy(s):
-        return pltpu.make_async_remote_copy(
-            src_ref=o_stage.at[s], dst_ref=o_buf.at[my_slot],
-            send_sem=o_send.at[s], recv_sem=o_recv.at[my_slot],
+        i = double * s + (1 - double) * (4 * lax.div(s, 2) + 2 * core + lax.rem(s, 2))
+        return lax.rem(z + near(i), RING)
+
+    def o_copy(s, n):
+        return pltpu.make_async_remote_copy(
+            src_ref=o_stage.at[s, n], dst_ref=o_buf.at[my_slot, n],
+            send_sem=o_send.at[s, n], recv_sem=o_recv.at[my_slot, n],
             device_id=(base + home(s), tp_base + owner), device_id_type=MESH,
         )
 
     def stays(s):
         return (home(s) == z) & (owner == core)
 
-    def finish(j, _):
+    def o_start(s, n):
+        @pl.when(stays(s))
+        def _():
+            pltpu.make_async_copy(
+                o_stage.at[s, n], o_buf.at[my_slot, n], o_recv.at[my_slot, n]
+            ).start()
+
+        @pl.when(jnp.logical_not(stays(s)))
+        def _():
+            o_copy(s, n).start()
+
+    def finish(j):
         out = (acc_all[j, :HEAD_DIM] / acc_all[j, HEAD_DIM : HEAD_DIM + 1]).T
-        for b in range(4):
-            block = out[b * IMG : (b + 1) * IMG]
-            both = jnp.concatenate([block[:HALF], block[HALF:]], axis=1)
-            o_stage[4 * j + b] = both.astype(jnp.bfloat16)
-        for b in range(4):
-            s = 4 * j + b
-
-            @pl.when(stays(s))
-            def _():
-                pltpu.make_async_copy(o_stage.at[s], o_buf.at[my_slot], o_recv.at[my_slot]).start()
-
-            @pl.when(jnp.logical_not(stays(s)))
-            def _():
-                o_copy(s).start()
-
-        return 0
-
-    lax.fori_loop(0, chunks, finish, 0)
-
+        for b in range(GROUP):
+            for n in range(2):
+                at = b * IMG + n * HALF
+                both = jnp.concatenate([out[at : at + ROWS], out[at + ROWS : at + HALF]], axis=1)
+                o_stage[GROUP * j + b, n] = both.astype(jnp.bfloat16)
+        for b in range(GROUP - 1, -1, -1):
+            o_start(GROUP * j + b, 0)
+
+    kv_last, value_last = arrive(RING // 2 - 1)
+
+    def last_chunks(k, _):
+        j = chunks - 1 - k
+        chunk_step(kv_last, value_last, j)
+        finish(j)
+        return 0
+
+    lax.fori_loop(0, chunks, last_chunks, 0)
+
+    def o_rest(k, _):
+        o_start(places - 1 - k, 1)
+        return 0
+
+    lax.fori_loop(0, places, o_rest, 0)
     limit = lax.div(HEADS + 3 - tp, 4)
-    for j in range(SLOTS):
-        pltpu.make_async_copy(o_buf.at[j], o_buf.at[j], o_recv.at[j]).wait()
-        valid = jnp.where(j < limit, 1.0, 0.0)
-        got = (o_buf[j].astype(jnp.float32) * valid).astype(jnp.bfloat16)
-        columns = slice(j * HEAD_DIM, (j + 1) * HEAD_DIM)
-        att_ref[:HALF, columns] = got[:, :HEAD_DIM]
-        att_ref[HALF:, columns] = got[:, HEAD_DIM:]
+
+    def gather(n):
+        for j in range(SLOTS):
+            pltpu.make_async_copy(o_buf.at[j, n], o_buf.at[j, n], o_recv.at[j, n]).wait()
+            valid = jnp.where(j < limit, 1.0, 0.0)
+            got = (o_buf[j, n].astype(jnp.float32) * valid).astype(jnp.bfloat16)
+            columns = slice(j * HEAD_DIM, (j + 1) * HEAD_DIM)
+            att_ref[n * HALF : n * HALF + ROWS, columns] = got[:, :HEAD_DIM]
+            att_ref[n * HALF + ROWS : (n + 1) * HALF, columns] = got[:, HEAD_DIM:]
 
     def pair_copy(n):
         return pltpu.make_async_remote_copy(
@@ -314,22 +348,28 @@
         )
 
     loads[4].wait()
-    for n in range(BLOCKS):
-        product = jnp.dot(
-            att_ref[n * ROWS : (n + 1) * ROWS], w_in[...], preferred_element_type=jnp.float32
-        ).astype(jnp.bfloat16)
-        for t in range(4):
-            part[n, t % 2, t // 2] = product[:, t * WIDE : (t + 1) * WIDE]
-        pair_copy(n).start()
-    for n in range(BLOCKS):
-        pair_copy(n).wait_recv()
-        both = part[n, core, 1 - side].astype(jnp.float32) + pair_in[n, 1 - side].astype(jnp.float32)
-        mate_out[n] = both.astype(jnp.bfloat16)
-        mate_copy(n).start()
     loads[3].wait()
     gates = gate_ref[...].astype(jnp.float32)
     chosen = lax.broadcasted_iota(jnp.int32, gates.shape, 0) == lax.div(pos, RING)
     gate_row = jnp.sum(jnp.where(chosen, gates, 0.0), axis=0, keepdims=True)
+
+    for half in range(2):
+        gather(half)
+        product = jnp.dot(
+            att_ref[half * HALF : (half + 1) * HALF], w_in[...], preferred_element_type=jnp.float32
+        ).astype(jnp.bfloat16)
+        blocks = (2 * half, 2 * half + 1)
+        for n in blocks:
+            rows = slice((n % 2) * ROWS, (n % 2 + 1) * ROWS)
+            for t in range(4):
+                part[n, t % 2, t // 2] = product[rows, t * WIDE : (t + 1) * WIDE]
+            pair_copy(n).start()
+        for n in blocks:
+            pair_copy(n).wait_recv()
+            both = part[n, core, 1 - side].astype(jnp.float32)
+            both += pair_in[n, 1 - side].astype(jnp.float32)
+            mate_out[n] = both.astype(jnp.bfloat16)
+            mate_copy(n).start()
     for n in range(BLOCKS):
         rows = slice(n * ROWS, (n + 1) * ROWS)
         both = part[n, core, side].astype(jnp.float32) + pair_in[n, side].astype(jnp.float32)
@@ -366,7 +406,8 @@
     def o_drain(s, _):
         @pl.when(jnp.logical_not(stays(s)))
         def _():
-            o_copy(s).wait_send()
+            o_copy(s, 0).wait_send()
+            o_copy(s, 1).wait_send()
 
         return 0
 
@@ -397,10 +438,10 @@
             pltpu.VMEM((RING, KEYS, PAIR), bf16),
             pltpu.VMEM((RING, HALF, PAIR), bf16),
             pltpu.VMEM((RING, IMG, PAIR), bf16),
-            pltpu.VMEM((4, 1, CHUNK), f32),
-            pltpu.VMEM((4, HEAD_DIM + 16, CHUNK), f32),
-            pltpu.VMEM((RING, HALF, PAIR), bf16),
-            pltpu.VMEM((SLOTS, HALF, PAIR), bf16),
+            pltpu.VMEM((2, 1, CHUNK), f32),
+            pltpu.VMEM((2, HEAD_DIM + 16, CHUNK), f32),
+            pltpu.VMEM((RING, 2, ROWS, PAIR), bf16),
+            pltpu.VMEM((SLOTS, 2, ROWS, PAIR), bf16),
             pltpu.VMEM((IMG, SLOTS * HEAD_DIM), bf16),
             pltpu.VMEM((BLOCKS, 2, 2, ROWS, WIDE), bf16),
             pltpu.VMEM((BLOCKS, 2, ROWS, WIDE), bf16),
@@ -408,7 +449,7 @@
             pltpu.VMEM((BLOCKS, ROWS, WIDE), bf16),
             sem((5,)),
             sem((RING,)), sem((RING,)), sem((RING,)), sem((RING,)),
-            sem((RING,)), sem((SLOTS,)), sem((RING,)),
+            sem((RING, 2)), sem((SLOTS, 2)), sem((RING,)),
             sem((BLOCKS,)), sem((BLOCKS,)), sem((BLOCKS,)), sem((BLOCKS,)),
         ],
         compiler_params=pltpu.CompilerParams(

time: 92.4 us -> 86.7 us (0.938)
  Pallas kernels: 89.8 us -> 84.2 us
    pallas_call x1, Pallas kernels: 89.8 us -> 84.2 us  [local(): pl.pallas_call(main_kernel, out_shape=jax.ShapeDtypeStruct(residual.shape...]
where the time goes in v3:
time: 86.7 us; the launch traced here: 85.9 us
  Pallas kernels  84.2 us (97%)
  local copies, waits for them, and re-layouts  1.66 us (2%)
    pallas_call x1, Pallas kernels, local(): pl.pallas_call(main_kernel, out_shape=jax.ShapeDtypeStruct(residual.shape...  84.2 us

profile of v3, /device:TPU:1, one launch (start us, length us, event | category | flops | bytes accessed | tf_op | source)
XLA Modules:
  0.0 85.9 jit_solution(12906112005075676359)
XLA Ops:
  0.0 84.2 %attend.1 = bf16[192,608]{1,0:T(8,128)(2,1)} custom-call(s32[8]{0:T(128)} %count_ref.1, bf16[192,640]{1,0:T(8,128)(2,1)} %q_hbm.1, bf16[224,640]{1,0:T(8,128)(2,1)} %k_hbm.1, bf16[224,640]{1,0:T(8,128)(2,1)} %v_hbm.1, f32[1,64]{1,0:T(1,128)} %bitcast.1, f32[2,64]{1,0:T(2,128)} %kg_ref.1, bf16[192,608]{1,0:T(8,128)(2,1)} %res_hbm.1, bf16[8,608]{1,0:T(8,128)(2,1)} %gate_ref.1, ...), custom_call_target="tpu_custom_call" | custom-call | tf_op jit(solution)/shard_map/attend/pallas_call | solution.py:425
  84.2 1.7 %copy.11 = bf16[192,608]{1,0:T(8,128)(2,1)} copy(bf16[192,608]{1,0:T(8,128)(2,1)} %attend.1) | data formatting | bytes 466944

commit v4 on v3

--- a/solution.py
+++ b/solution.py
@@ -17,8 +17,9 @@
 CHUNK = GROUP * IMG
 STEP = 2 * KEYS
 WIDE = 608
-BLOCKS = 4
+BLOCKS = 3
 ROWS = IMG // BLOCKS
+PIECES = ((0, 64), (128, 32))
 LOG2E = 1.4426950408889634
 MESH = pl.DeviceIdType.MESH
 epsilon = 1e-06
@@ -91,11 +92,13 @@
 def main_kernel(
     count_ref, q_hbm, k_hbm, v_hbm, qg_ref, kg_ref, res_hbm, gate_ref, w_hbm, out_ref,
     q_in, k_in, v_in, res_in, w_in, qp_ref, kvp_ref,
-    kv_buf, q_buf, q_all, m_all, acc_all, o_stage, o_buf, att_ref,
+    kv_buf, q_buf, q_all, m_all, acc_all,
+    o_stage_a, o_stage_b, o_buf_a, o_buf_b, att_ref,
     part, pair_in, mate_out, mate_in, load,
     kv_send, kv_recv, q_send, q_recv, o_send, o_recv, relay_send,
     pair_send, pair_recv, mate_send, mate_recv,
 ):
+    o_stage, o_buf = (o_stage_a, o_stage_b), (o_buf_a, o_buf_b)
     pos = lax.axis_index("seq")
     tp = lax.axis_index("tp")
     z = lax.rem(pos, RING)
@@ -107,15 +110,6 @@
     mate = (pos, 2 * (1 - side) + core)
     sibling = (pos, tp_base + 1 - core)
 
-    loads = [
-        pltpu.make_async_copy(source, place, load.at[n])
-        for n, (source, place) in enumerate(
-            [(q_hbm, q_in), (k_hbm, k_in), (v_hbm, v_in), (res_hbm, res_in), (w_hbm, w_in)]
-        )
-    ]
-    for copy in loads:
-        copy.start()
-
     barrier = pltpu.get_barrier_semaphore()
     linear = z * 2 + core
 
@@ -129,8 +123,18 @@
         )
         return 0
 
-    lax.fori_loop(1, 2 * RING, greet, 0)
+    for low, high in ((8, 25), (1, 8), (25, 32)):
+        lax.fori_loop(low, high, greet, 0)
     pl.semaphore_signal(barrier, inc=1, device_id=mate, device_id_type=MESH)
+    loads = [
+        pltpu.make_async_copy(source, place, load.at[n])
+        for n, (source, place) in enumerate(
+            [(q_hbm, q_in), (k_hbm, k_in), (v_hbm, v_in), (res_hbm, res_in), (w_hbm, w_in)]
+        )
+    ]
+    for copy in loads:
+        copy.start()
+
     count = count_ref[lax.div(pos, RING)]
     loads[0].wait()
     pack_queries(q_in, qg_ref, qp_ref)
@@ -205,6 +209,8 @@
     kv_pass(1)
     q_pass(0)
     kv_pass(0)
+
+    loads[4].wait()
 
     def relay(i):
         return pltpu.make_async_remote_copy(
@@ -278,7 +284,7 @@
 
     def o_copy(s, n):
         return pltpu.make_async_remote_copy(
-            src_ref=o_stage.at[s, n], dst_ref=o_buf.at[my_slot, n],
+            src_ref=o_stage[n].at[s], dst_ref=o_buf[n].at[my_slot],
             send_sem=o_send.at[s, n], recv_sem=o_recv.at[my_slot, n],
             device_id=(base + home(s), tp_base + owner), device_id_type=MESH,
         )
@@ -290,7 +296,7 @@
         @pl.when(stays(s))
         def _():
             pltpu.make_async_copy(
-                o_stage.at[s, n], o_buf.at[my_slot, n], o_recv.at[my_slot, n]
+                o_stage[n].at[s], o_buf[n].at[my_slot], o_recv.at[my_slot, n]
             ).start()
 
         @pl.when(jnp.logical_not(stays(s)))
@@ -300,10 +306,10 @@
     def finish(j):
         out = (acc_all[j, :HEAD_DIM] / acc_all[j, HEAD_DIM : HEAD_DIM + 1]).T
         for b in range(GROUP):
-            for n in range(2):
-                at = b * IMG + n * HALF
-                both = jnp.concatenate([out[at : at + ROWS], out[at + ROWS : at + HALF]], axis=1)
-                o_stage[GROUP * j + b, n] = both.astype(jnp.bfloat16)
+            for n, (first, size) in enumerate(PIECES):
+                at = b * IMG + first
+                both = [out[at : at + size], out[at + size : at + 2 * size]]
+                o_stage[n][GROUP * j + b] = jnp.concatenate(both, axis=1).astype(jnp.bfloat16)
         for b in range(GROUP - 1, -1, -1):
             o_start(GROUP * j + b, 0)
 
@@ -325,13 +331,14 @@
     limit = lax.div(HEADS + 3 - tp, 4)
 
     def gather(n):
+        first, size = PIECES[n]
         for j in range(SLOTS):
-            pltpu.make_async_copy(o_buf.at[j, n], o_buf.at[j, n], o_recv.at[j, n]).wait()
+            pltpu.make_async_copy(o_buf[n].at[j], o_buf[n].at[j], o_recv.at[j, n]).wait()
             valid = jnp.where(j < limit, 1.0, 0.0)
-            got = (o_buf[j, n].astype(jnp.float32) * valid).astype(jnp.bfloat16)
+            got = (o_buf[n][j].astype(jnp.float32) * valid).astype(jnp.bfloat16)
             columns = slice(j * HEAD_DIM, (j + 1) * HEAD_DIM)
-            att_ref[n * HALF : n * HALF + ROWS, columns] = got[:, :HEAD_DIM]
-            att_ref[n * HALF + ROWS : (n + 1) * HALF, columns] = got[:, HEAD_DIM:]
+            att_ref[first : first + size, columns] = got[:, :HEAD_DIM]
+            att_ref[first + size : first + 2 * size, columns] = got[:, HEAD_DIM:]
 
     def pair_copy(n):
         return pltpu.make_async_remote_copy(
@@ -347,22 +354,22 @@
             device_id=mate, device_id_type=MESH,
         )
 
-    loads[4].wait()
     loads[3].wait()
     gates = gate_ref[...].astype(jnp.float32)
     chosen = lax.broadcasted_iota(jnp.int32, gates.shape, 0) == lax.div(pos, RING)
     gate_row = jnp.sum(jnp.where(chosen, gates, 0.0), axis=0, keepdims=True)
 
-    for half in range(2):
-        gather(half)
+    for piece, blocks in ((0, (0, 1)), (1, (2,))):
+        gather(piece)
+        first, size = PIECES[piece]
         product = jnp.dot(
-            att_ref[half * HALF : (half + 1) * HALF], w_in[...], preferred_element_type=jnp.float32
-        ).astype(jnp.bfloat16)
-        blocks = (2 * half, 2 * half + 1)
+            att_ref[first : first + 2 * size], w_in[...], preferred_element_type=jnp.float32
+        )
         for n in blocks:
-            rows = slice((n % 2) * ROWS, (n % 2 + 1) * ROWS)
+            rows = slice(n * ROWS - first, (n + 1) * ROWS - first)
             for t in range(4):
-                part[n, t % 2, t // 2] = product[rows, t * WIDE : (t + 1) * WIDE]
+                share = product[rows, t * WIDE : (t + 1) * WIDE]
+                part[n, t % 2, t // 2] = share.astype(jnp.bfloat16)
             pair_copy(n).start()
         for n in blocks:
             pair_copy(n).wait_recv()
@@ -440,8 +447,10 @@
             pltpu.VMEM((RING, IMG, PAIR), bf16),
             pltpu.VMEM((2, 1, CHUNK), f32),
             pltpu.VMEM((2, HEAD_DIM + 16, CHUNK), f32),
-            pltpu.VMEM((RING, 2, ROWS, PAIR), bf16),
-            pltpu.VMEM((SLOTS, 2, ROWS, PAIR), bf16),
+            pltpu.VMEM((RING, PIECES[0][1], PAIR), bf16),
+            pltpu.VMEM((RING, PIECES[1][1], PAIR), bf16),
+            pltpu.VMEM((SLOTS, PIECES[0][1], PAIR), bf16),
+            pltpu.VMEM((SLOTS, PIECES[1][1], PAIR), bf16),
             pltpu.VMEM((IMG, SLOTS * HEAD_DIM), bf16),
             pltpu.VMEM((BLOCKS, 2, 2, ROWS, WIDE), bf16),
             pltpu.VMEM((BLOCKS, 2, ROWS, WIDE), bf16),

time: 86.7 us -> 86.8 us (level)
  no operation moved by 1% of the time
where the time goes in v4:
time: 86.8 us; the launch traced here: 86.6 us
  Pallas kernels  84.9 us (98%)
  local copies, waits for them, and re-layouts  1.66 us (2%)
    pallas_call x1, Pallas kernels, local(): pl.pallas_call(main_kernel, out_shape=jax.ShapeDtypeStruct(residual.shape...  84.9 us

profile of v4, /device:TPU:1, one launch (start us, length us, event | category | flops | bytes accessed | tf_op | source)
XLA Modules:
  0.0 86.6 jit_solution(701722241774970317)
XLA Ops:
  0.0 84.9 %attend.1 = bf16[192,608]{1,0:T(8,128)(2,1)} custom-call(s32[8]{0:T(128)} %count_ref.1, bf16[192,640]{1,0:T(8,128)(2,1)} %q_hbm.1, bf16[224,640]{1,0:T(8,128)(2,1)} %k_hbm.1, bf16[224,640]{1,0:T(8,128)(2,1)} %v_hbm.1, f32[1,64]{1,0:T(1,128)} %bitcast.1, f32[2,64]{1,0:T(2,128)} %kg_ref.1, bf16[192,608]{1,0:T(8,128)(2,1)} %res_hbm.1, bf16[8,608]{1,0:T(8,128)(2,1)} %gate_ref.1, ...), custom_call_target="tpu_custom_call" | custom-call | tf_op jit(solution)/shard_map/attend/pallas_call | solution.py:432
  84.9 1.7 %copy.11 = bf16[192,608]{1,0:T(8,128)(2,1)} copy(bf16[192,608]{1,0:T(8,128)(2,1)} %attend.1) | data formatting | bytes 466944

commit v5 on v4

--- a/solution.py
+++ b/solution.py
@@ -123,6 +123,7 @@
         )
         return 0
 
+    pltpu.make_async_copy(q_hbm, q_in, load.at[0]).start()
     for low, high in ((8, 25), (1, 8), (25, 32)):
         lax.fori_loop(low, high, greet, 0)
     pl.semaphore_signal(barrier, inc=1, device_id=mate, device_id_type=MESH)
@@ -132,7 +133,7 @@
             [(q_hbm, q_in), (k_hbm, k_in), (v_hbm, v_in), (res_hbm, res_in), (w_hbm, w_in)]
         )
     ]
-    for copy in loads:
+    for copy in loads[1:]:
         copy.start()
 
     count = count_ref[lax.div(pos, RING)]
@@ -232,9 +233,9 @@
         q_all[s, HALF:] = jnp.where(first, pltpu.roll(packed, HEAD_DIM, 1), 0.0).astype(jnp.bfloat16)
         return 0
 
-    lax.fori_loop(0, places, unpack, 0)
     m_all[...] = jnp.full_like(m_all, -jnp.inf)
     acc_all[...] = jnp.zeros_like(acc_all)
+    lax.fori_loop(0, places, unpack, 0)
 
     def arrive(i):
         for n in range(2):

time: 86.8 us -> 86.8 us (level)
  no operation moved by 1% of the time
where the time goes in v5:
time: 86.8 us; the launch traced here: 86.6 us
  Pallas kernels  84.9 us (98%)
  local copies, waits for them, and re-layouts  1.66 us (2%)
    pallas_call x1, Pallas kernels, local(): pl.pallas_call(main_kernel, out_shape=jax.ShapeDtypeStruct(residual.shape...  84.9 us

profile of v5, /device:TPU:1, one launch (start us, length us, event | category | flops | bytes accessed | tf_op | source)
XLA Modules:
  0.0 86.6 jit_solution(1454847714512875113)
XLA Ops:
  0.0 84.9 %attend.1 = bf16[192,608]{1,0:T(8,128)(2,1)} custom-call(s32[8]{0:T(128)} %count_ref.1, bf16[192,640]{1,0:T(8,128)(2,1)} %q_hbm.1, bf16[224,640]{1,0:T(8,128)(2,1)} %k_hbm.1, bf16[224,640]{1,0:T(8,128)(2,1)} %v_hbm.1, f32[1,64]{1,0:T(1,128)} %bitcast.1, f32[2,64]{1,0:T(2,128)} %kg_ref.1, bf16[192,608]{1,0:T(8,128)(2,1)} %res_hbm.1, bf16[8,608]{1,0:T(8,128)(2,1)} %gate_ref.1, ...), custom_call_target="tpu_custom_call" | custom-call | tf_op jit(solution)/shard_map/attend/pallas_call | solution.py:433
  84.9 1.7 %copy.11 = bf16[192,608]{1,0:T(8,128)(2,1)} copy(bf16[192,608]{1,0:T(8,128)(2,1)} %attend.1) | data formatting | bytes 466944
